TPU v7x, 256 devices: a whole 4x4x8 slice. The times are simulated.
256 devices in a mesh: ta: 4 (over y), ha: 16 (over x, z_hi, core), wa: 4 (over z_lo).
Axes of the slice: x: 4, y: 4, z: 8 (z_hi: 2, z_lo: 4; z = z_hi * 4 + z_lo), core: 2. Of those that a mesh axis runs over, the one named last changes fastest.
Arguments:
- latents: bfloat16 [8, 256, 128, 256], P('ta', 'ha', 'wa'), may hold values from -6 to 6
- norm_gain: float32 [256], replicated, may hold values from 0.1 to 1.9
- conv_weight: bfloat16 [3, 3, 3, 256, 256], replicated, may hold values from -0.078125 to 0.078125
- qkv_weight: bfloat16 [1024, 16, 3, 128], P(None, ('ta', 'wa')), may hold values from -2.7 to 2.7
Outputs:
- block_out: bfloat16 [8, 256, 128, 256], P('ta', 'ha', 'wa')
- attended: bfloat16 [8, 128, 64, 16, 128], P(None, 'ha', None, ('ta', 'wa'))
All inputs are finite; a program needn't handle non-finite values.
Results may differ from a plain program's by a relative error of at most 0.0062.
Values may be sent and summed in bfloat16 or wider, within the bound.
No kernel may reach another device: no remote copies, remote signals or barrier semaphores. Data moves between devices by JAX's collectives and lax.ppermute only.
A program may use at most 128 MiB of HBM per device.

v0:
```python
import jax
import jax.numpy as jnp
from jax import lax
from jax.sharding import PartitionSpec as P

WIN = 4


def extended(cells, sides, width):
    for axis, dim in sides:
        count = lax.axis_size(axis)
        ends = count - 1
        head = lax.slice_in_dim(cells, 0, width, axis=dim)
        tail = lax.slice_in_dim(cells, cells.shape[dim] - width, cells.shape[dim], axis=dim)
        cells = jnp.concatenate(
            [
                lax.ppermute(tail, axis, [(i, (i + 1) % count) for i in range(ends)]),
                cells,
                lax.ppermute(head, axis, [((i + 1) % count, i) for i in range(ends)]),
            ],
            axis=dim,
        )
    return cells


def local(latents, norm_gain, conv_weight, qkv_weight):
    t_dev, h_dev, w_dev, channels = latents.shape
    rows_dev = h_dev // 2
    cols_dev = w_dev // 2
    latent_f32 = latents.astype(jnp.float32)
    scale_rms = lax.rsqrt(jnp.mean(latent_f32 * latent_f32, axis=-1, keepdims=True) + 1e-06)
    normed = jax.nn.silu(latent_f32 * scale_rms * norm_gain).astype(jnp.bfloat16)
    padded = extended(normed, (("ta", 0), ("ha", 1), ("wa", 2)), 1)
    conv_out = lax.conv_general_dilated(
        padded[None],
        conv_weight,
        (1, 1, 1),
        "VALID",
        dimension_numbers=("NDHWC", "DHWIO", "NDHWC"),
        preferred_element_type=jnp.float32,
    )[0]
    block_out = (latent_f32 + conv_out).astype(jnp.bfloat16)
    width_in, head_dev, qkv_count, head_size = qkv_weight.shape
    col_heads = lax.all_gather(qkv_weight, "ta", axis=1, tiled=True)
    heads = col_heads.shape[1]
    wide = lax.all_gather(block_out, "wa", axis=2, tiled=True)
    patch_cols = wide.shape[2] // 2
    patches = (
        wide.reshape(t_dev, rows_dev, 2, patch_cols, 2, channels)
        .transpose(0, 1, 3, 2, 4, 5)
        .reshape(t_dev * rows_dev * patch_cols, 4 * channels)
    )
    projected = jnp.dot(
        patches, col_heads.reshape(width_in, -1), preferred_element_type=jnp.float32
    ).astype(jnp.bfloat16)
    qkv_rows = projected.reshape(t_dev, rows_dev, patch_cols, heads, qkv_count, head_size)
    queries = qkv_rows[:, :, :, :, 0, :]
    key_value = qkv_rows[:, :, :, :, 1:, :].reshape(
        t_dev, rows_dev, patch_cols, heads, 2 * head_size
    )
    kv_rim = extended(key_value, (("ha", 1),), WIN)
    row_base = lax.axis_index("ha") * rows_dev
    total_rows = rows_dev * lax.axis_size("ha")

    def attend(block_idx):
        q_block = lax.dynamic_slice_in_dim(queries, block_idx * WIN, WIN, 1)
        kv_block = lax.dynamic_slice_in_dim(kv_rim, block_idx * WIN, 3 * WIN, 1)
        key_part = kv_block[..., :head_size]
        value_part = kv_block[..., head_size:]
        scores = jnp.einsum(
            "tiahd,tjbhd->thiajb", q_block, key_part, preferred_element_type=jnp.float32
        ) * head_size ** (-0.5)
        q_row = jnp.arange(WIN, dtype=jnp.int32)[:, None]
        k_row = jnp.arange(3 * WIN, dtype=jnp.int32)[None, :] - WIN
        k_global = row_base + block_idx * WIN + k_row
        allowed = (jnp.abs(q_row - k_row) <= WIN) & (k_global >= 0) & (k_global < total_rows)
        scores = jnp.where(allowed[None, None, :, None, :, None], scores, -1e30)
        row_max = jnp.max(scores, axis=(4, 5), keepdims=True)
        exp_scores = jnp.exp(scores - row_max)
        probs = (exp_scores / jnp.sum(exp_scores, axis=(4, 5), keepdims=True)).astype(jnp.bfloat16)
        result = jnp.einsum(
            "thiajb,tjbhd->tiahd", probs, value_part, preferred_element_type=jnp.float32
        )
        return result.astype(jnp.bfloat16)

    blocks = lax.map(attend, jnp.arange(rows_dev // WIN, dtype=jnp.int32))
    attended = blocks.transpose(1, 0, 2, 3, 4, 5).reshape(
        t_dev, rows_dev, patch_cols, heads, head_size
    )
    attended = lax.all_to_all(attended, "ta", split_axis=3, concat_axis=0, tiled=True)
    return (block_out, attended)


def solution(mesh):
    return jax.shard_map(
        local,
        mesh=mesh,
        in_specs=(P("ta", "ha", "wa", None), P(), P(), P(None, ("ta", "wa"), None, None)),
        out_specs=(P("ta", "ha", "wa", None), P(None, "ha", None, ("ta", "wa"), None)),
        check_vma=False,
    )
```

profile of v0, /device:TPU:67, one launch (start us, length us, event | category | flops | bytes accessed | tf_op | source)
XLA Modules:
  0.0 310.4 jit_solution(17546351096016199151)
XLA Ops:
  18.6 3.8 %collective-permute-done.1 = bf16[1,16,32,256]{3,1,2,0:T(8,128)(2,1)S(1)} collective-permute-done((bf16[1,16,32,256]{3,1,2,0:T(8,128)(2,1)S(1)}, bf16[1,16,32,256]{3,1,2,0:T(8,128)(2,1)S(1)}, u32[]{:S(2)}, u32[]{:S(2)}) %collective-permute-start.1) | collective-permute-done | bytes 262176 | tf_op jit(solution)/shard_map/ppermute | solution.py:19
  22.6 8.7 %collective-permute-start.2 = (bf16[4,1,32,256]{3,1,2,0:T(2,128)(2,1)S(1)}, bf16[4,1,32,256]{3,1,2,0:T(2,128)(2,1)S(1)}, u32[]{:S(2)}, u32[]{:S(2)}) collective-permute-start(bf16[4,1,32,256]{3,1,2,0:T(2,128)(2,1)S(1)} %get-tuple-element.124), channel_id=1, source_target_pairs={{0,4},{4,8},{8,12},{12,16},{16,20},{20,24},{24,28},{28,32},{32,36}... | collective-permute-start | bytes 196616 | tf_op jit(solution)/shard_map/ppermute | solution.py:17
  33.9 9.1 %collective-permute-done.3 = bf16[4,1,32,256]{3,1,2,0:T(2,128)(2,1)S(1)} collective-permute-done((bf16[4,1,32,256]{3,1,2,0:T(2,128)(2,1)S(1)}, bf16[4,1,32,256]{3,1,2,0:T(2,128)(2,1)S(1)}, u32[]{:S(2)}, u32[]{:S(2)}) %collective-permute-start.3) | collective-permute-done | bytes 65568 | tf_op jit(solution)/shard_map/ppermute | solution.py:19
  52.6 5.0 %fusion.23 = f32[2,16,8,5,256]{4,2,3,1,0:T(8,128)S(1)} fusion(bf16[3,3,3,256,256]{4,3,2,1,0:T(8,128)(2,1)S(1)} %copy-done, bf16[4,18,1,7,2,256]{5,3,4,1,0,2:T(8,128)(2,1)S(1)} %slice.56, bf16[4,18,1,8,5,256]{5,3,4,1,0,2:T(8,128)(2,1)S(1)} %copy.44, pred[8,5]{0,1:T(8,128)(4,1)S(1)} %copy-done.6), kind=kOutput, calls=%fused_computation.40 | convolution fusion | flops 4536369152 | bytes 6840360 | tf_op jit(solution)/shard_map/conv_general_dilated | solution.py:34
  60.0 46.3 %all-gather.3.cloned.1.call-done = bf16[2,16,128,256]{3,1,2,0:T(8,128)(2,1)} async-done(((bf16[2,16,32,256]{3,1,2,0:T(8,128)(2,1)}), bf16[2,16,128,256]{3,1,2,0:T(8,128)(2,1)}) %all-gather.3.cloned.1.call-update) | async-done | bytes 2097168 | tf_op jit(solution)/shard_map/all_gather | solution.py:46
  112.6 4.5 %reshape.105 = bf16[1024,1024]{1,0:T(8,128)(2,1)} reshape(bf16[2,8,64,2,2,256]{5,4,3,2,1,0:T(2,128)(2,1)} %bitcast.88) | data formatting | bytes 4194304 | tf_op jit(solution)/shard_map/reshape | solution.py:51
  117.0 33.7 %all-gather.5.cloned.1.call-done = bf16[1024,4,3,128]{3,0,2,1:T(8,128)(2,1)} async-done(((bf16[1024,1,3,128]{3,0,2,1:T(8,128)(2,1)}), bf16[1024,4,3,128]{3,0,2,1:T(8,128)(2,1)}) %all-gather.5.cloned.1.call-update) | async-done | bytes 3145744 | tf_op jit(solution)/shard_map/all_gather | solution.py:44
  150.7 4.6 %copy.47 = bf16[1024,4,3,128]{0,3,2,1:T(8,128)(2,1)} copy(bf16[1024,4,3,128]{3,0,2,1:T(8,128)(2,1)} %all-gather.5.cloned.1.call-done) | data formatting | bytes 6291456 | tf_op jit(solution)/shard_map/all_gather | solution.py:44
  155.4 6.0 %convolution_convert_fusion = bf16[1024,1536]{1,0:T(8,128)(2,1)S(1)} fusion(bf16[1024,1024]{1,0:T(8,128)(2,1)} %reshape.105, bf16[1024,1536]{0,1:T(8,128)(2,1)} %bitcast.91), kind=kOutput, calls=%fused_computation.28 | convolution fusion | flops 3222798336 | bytes 8388608 | tf_op jit(solution)/shard_map/dot_general | solution.py:53
  161.3 4.5 %reshape.107 = bf16[2,8,64,4,3,128]{5,4,3,2,1,0:T(4,128)(2,1)} reshape(bf16[1024,1536]{1,0:T(8,128)(2,1)S(1)} %convolution_convert_fusion) | data formatting | bytes 6291456 | tf_op jit(solution)/shard_map/reshape | solution.py:56
  165.9 4.6 %slice.58 = bf16[2,8,64,4,2,128]{5,4,3,2,1,0:T(2,128)(2,1)S(1)} slice(bf16[2,8,64,4,3,128]{5,4,3,2,1,0:T(4,128)(2,1)} %reshape.107), slice={[0:2], [0:8], [0:64], [0:4], [1:3], [0:128]} | slice | bytes 4194304 | tf_op jit(solution)/shard_map/slice | solution.py:58
  176.7 6.3 %collective-permute-start.6 = (bf16[2,4,64,4,256]{4,2,1,3,0:T(8,128)(2,1)}, bf16[2,4,64,4,256]{4,2,1,3,0:T(8,128)(2,1)}, u32[]{:S(2)}, u32[]{:S(2)}) collective-permute-start(bf16[2,4,64,4,256]{4,2,1,3,0:T(8,128)(2,1)} %get-tuple-element.120), channel_id=1, source_target_pairs={{0,4},{4,8},{8,12},{12,16},{16,20},{20,24},{24,28},{28,32},{32,36}... | collective-permute-start | bytes 3145736 | tf_op jit(solution)/shard_map/ppermute | solution.py:17
  185.2 3.8 %slice.61 = bf16[2,8,64,4,1,128]{5,4,3,2,1,0:T(2,128)(2,1)S(1)} slice(bf16[2,8,64,4,3,128]{5,4,3,2,1,0:T(4,128)(2,1)} %reshape.107), slice={[0:2], [0:8], [0:64], [0:4], [0:1], [0:128]} | slice | bytes 2097152 | tf_op jit(solution)/shard_map/slice | solution.py:57
  189.3 37.8 %collective-permute-done.6 = bf16[2,4,64,4,256]{4,2,1,3,0:T(8,128)(2,1)} collective-permute-done((bf16[2,4,64,4,256]{4,2,1,3,0:T(8,128)(2,1)}, bf16[2,4,64,4,256]{4,2,1,3,0:T(8,128)(2,1)}, u32[]{:S(2)}, u32[]{:S(2)}) %collective-permute-start.6) | collective-permute-done | bytes 1048608 | tf_op jit(solution)/shard_map/ppermute | solution.py:17
  227.0 4.6 %collective-permute-done.7 = bf16[2,4,64,4,256]{4,2,1,3,0:T(8,128)(2,1)} collective-permute-done((bf16[2,4,64,4,256]{4,2,1,3,0:T(8,128)(2,1)}, bf16[2,4,64,4,256]{4,2,1,3,0:T(8,128)(2,1)}, u32[]{:S(2)}, u32[]{:S(2)}) %collective-permute-start.7) | collective-permute-done | bytes 1048608 | tf_op jit(solution)/shard_map/ppermute | solution.py:19
  235.0 44.8 %while.12 = (s32[]{:T(128)}, bf16[2,2,4,64,4,128]{5,3,4,2,0,1:T(8,128)(2,1)}, s32[2]{0:T(128)S(1)}, bf16[2,16,64,4,256]{4,2,1,3,0:T(8,128)(2,1)}, s32[]{:T(128)}...) while((s32[]{:T(128)}, ...), condition=%wide.region_4.5_spmd, body=%wide.region_1.4_spmd.sunk | while | flops 824439104 | bytes 64005228 | solution.py:86
  236.3 3.7 %fusion.49 = (f32[2,4,4,64]{3,2,1,0:T(4,128)S(1)}, f32[2,4,4,64,12,64]{3,5,4,2,1,0:T(8,128)S(1)}) fusion(pred[4,12]{1,0:T(4,128)(4,1)S(1)} %fusion.48, bf16[2,16,64,4,256]{4,2,1,3,0:T(8,128)(2,1)} %get-tuple-element.200, s32[]{:T(128)S(6)} %select_n.43, bf16[2,8,64,4,128]{4,2,1,3,0:T(8,128)(2,1)S(1)} %get-tuple-element.202, s32[]{:T(128)S(6)} %select_n.44), kind=kOutput, calls=%fused_computation.3.clone.1 | convolution fusion | flops 407369728 | bytes 8397320 | tf_op jit(solution)/shard_map/while/body/eval_jaxpr/tiahd,tjbhd->thiajb/dot_general | solution.py:70
  240.0 4.5 %copy-done.2 = f32[2,4,4,64,12,64]{3,5,4,2,1,0:T(8,128)} copy-done((f32[2,4,4,64,12,64]{3,5,4,2,1,0:T(8,128)}, f32[2,4,4,64,12,64]{3,5,4,2,1,0:T(8,128)S(1)}, u32[]{:S(2)}) %copy-start.2) | copy-done | bytes 6291480 | tf_op jit(solution)/shard_map/while
  248.0 8.4 %fusion.51 = bf16[1,2,4,64,4,128]{5,3,2,4,1,0:T(8,128)(2,1)S(1)} fusion(f32[2,4,4,64,12,64]{3,5,4,2,1,0:T(8,128)} %copy-done.2, f32[2,4,4,64]{3,2,1,0:T(4,128)S(1)} %fusion.50, f32[2,4,4,64]{3,2,1,0:T(4,128)S(1)} %get-tuple-element.172, pred[4,12]{1,0:T(4,128)(4,1)S(1)} %fusion.48, bf16[2,16,64,4,256]{4,2,1,3,0:T(8,128)(2,1)} %get-tuple-element.200, ...), kind=kOutput, calls=%fused_computation.11.clone.1 | convolution fusion | flops 410779648 | bytes 14696504 | tf_op jit(solution)/shard_map/while/body/eval_jaxpr/thiajb,tjbhd->tiahd/dot_general | solution.py:81
  258.7 3.7 %fusion.49 = (f32[2,4,4,64]{3,2,1,0:T(4,128)S(1)}, f32[2,4,4,64,12,64]{3,5,4,2,1,0:T(8,128)S(1)}) fusion(pred[4,12]{1,0:T(4,128)(4,1)S(1)} %fusion.48, bf16[2,16,64,4,256]{4,2,1,3,0:T(8,128)(2,1)} %get-tuple-element.200, s32[]{:T(128)S(6)} %select_n.43, bf16[2,8,64,4,128]{4,2,1,3,0:T(8,128)(2,1)S(1)} %get-tuple-element.202, s32[]{:T(128)S(6)} %select_n.44), kind=kOutput, calls=%fused_computation.3.clone.1 | convolution fusion | flops 407369728 | bytes 8397320 | tf_op jit(solution)/shard_map/while/body/eval_jaxpr/tiahd,tjbhd->thiajb/dot_general | solution.py:70
  262.4 4.5 %copy-done.2 = f32[2,4,4,64,12,64]{3,5,4,2,1,0:T(8,128)} copy-done((f32[2,4,4,64,12,64]{3,5,4,2,1,0:T(8,128)}, f32[2,4,4,64,12,64]{3,5,4,2,1,0:T(8,128)S(1)}, u32[]{:S(2)}) %copy-start.2) | copy-done | bytes 6291480 | tf_op jit(solution)/shard_map/while
  270.4 8.4 %fusion.51 = bf16[1,2,4,64,4,128]{5,3,2,4,1,0:T(8,128)(2,1)S(1)} fusion(f32[2,4,4,64,12,64]{3,5,4,2,1,0:T(8,128)} %copy-done.2, f32[2,4,4,64]{3,2,1,0:T(4,128)S(1)} %fusion.50, f32[2,4,4,64]{3,2,1,0:T(4,128)S(1)} %get-tuple-element.172, pred[4,12]{1,0:T(4,128)(4,1)S(1)} %fusion.48, bf16[2,16,64,4,256]{4,2,1,3,0:T(8,128)(2,1)} %get-tuple-element.200, ...), kind=kOutput, calls=%fused_computation.11.clone.1 | convolution fusion | flops 410779648 | bytes 14696504 | tf_op jit(solution)/shard_map/while/body/eval_jaxpr/thiajb,tjbhd->tiahd/dot_general | solution.py:81
  282.3 4.2 %all-to-all-start = ((bf16[2,8,64,4,128]{4,2,1,0,3:T(8,128)(2,1)}), bf16[2,8,64,4,128]{4,2,1,0,3:T(8,128)(2,1)}, u32[]{:S(2)}, u32[]{:S(2)}) async-start(bf16[2,8,64,4,128]{4,2,1,0,3:T(8,128)(2,1)} %copy.54), calls=%async_computation | async-start | bytes 2097152 | tf_op jit(solution)/shard_map/all_to_all | solution.py:90
  288.5 12.7 %all-to-all-done = bf16[2,8,64,4,128]{4,2,1,0,3:T(8,128)(2,1)} async-done(((bf16[2,8,64,4,128]{4,2,1,0,3:T(8,128)(2,1)}), bf16[2,8,64,4,128]{4,2,1,0,3:T(8,128)(2,1)}, u32[]{:S(2)}, u32[]{:S(2)}) %all-to-all-start) | async-done | bytes 1048608 | tf_op jit(solution)/shard_map/all_to_all | solution.py:90
  (69 shorter events, 61.1 us)
Async XLA Ops:
  7.2 45.4 %copy-start = (bf16[3,3,3,256,256]{4,3,2,1,0:T(8,128)(2,1)S(1)}, bf16[3,3,3,256,256]{4,3,2,1,0:T(8,128)(2,1)}, u32[]{:S(2)}) copy-start(bf16[3,3,3,256,256]{4,3,2,1,0:T(8,128)(2,1)} %param.8) | copy-start | bytes 10616836
  7.2 99.1 %all-gather.3.cloned.1.call-start = ((), (), s32[]{:S(2)}) async-start(), calls=%async_computation.1 | async-start | bytes 2621440 | tf_op jit(solution)/shard_map/all_gather | solution.py:46
  10.4 8.2 %collective-permute-start = (bf16[1,16,32,256]{3,1,2,0:T(8,128)(2,1)S(1)}, bf16[1,16,32,256]{3,1,2,0:T(8,128)(2,1)S(1)}, u32[]{:S(2)}, u32[]{:S(2)}) collective-permute-start(bf16[1,16,32,256]{3,1,2,0:T(8,128)(2,1)S(1)} %get-tuple-element.126), channel_id=1, source_target_pairs={{0,64},{64,128},{128,192},{1,65},{65,129},{129,193},{2,66},{66,130... | collective-permute-start | bytes 786440 | tf_op jit(solution)/shard_map/ppermute | solution.py:17
  13.6 8.8 %collective-permute-start.1 = (bf16[1,16,32,256]{3,1,2,0:T(8,128)(2,1)S(1)}, bf16[1,16,32,256]{3,1,2,0:T(8,128)(2,1)S(1)}, u32[]{:S(2)}, u32[]{:S(2)}) collective-permute-start(bf16[1,16,32,256]{3,1,2,0:T(8,128)(2,1)S(1)} %get-tuple-element.127), channel_id=1, source_target_pairs={{64,0},{128,64},{192,128},{65,1},{129,65},{193,129},{66,2},{130,66... | collective-permute-start | bytes 786440 | tf_op jit(solution)/shard_map/ppermute | solution.py:19
  22.6 11.2 %collective-permute-start.2 = (bf16[4,1,32,256]{3,1,2,0:T(2,128)(2,1)S(1)}, bf16[4,1,32,256]{3,1,2,0:T(2,128)(2,1)S(1)}, u32[]{:S(2)}, u32[]{:S(2)}) collective-permute-start(bf16[4,1,32,256]{3,1,2,0:T(2,128)(2,1)S(1)} %get-tuple-element.124), channel_id=1, source_target_pairs={{0,4},{4,8},{8,12},{12,16},{16,20},{20,24},{24,28},{28,32},{32,36}... | collective-permute-start | bytes 196616 | tf_op jit(solution)/shard_map/ppermute | solution.py:17
  31.4 11.6 %collective-permute-start.3 = (bf16[4,1,32,256]{3,1,2,0:T(2,128)(2,1)S(1)}, bf16[4,1,32,256]{3,1,2,0:T(2,128)(2,1)S(1)}, u32[]{:S(2)}, u32[]{:S(2)}) collective-permute-start(bf16[4,1,32,256]{3,1,2,0:T(2,128)(2,1)S(1)} %get-tuple-element.125), channel_id=1, source_target_pairs={{4,0},{8,4},{12,8},{16,12},{20,16},{24,20},{28,24},{32,28},{36,32}... | collective-permute-start | bytes 196616 | tf_op jit(solution)/shard_map/ppermute | solution.py:19
  43.0 5.3 %collective-permute-start.4 = (bf16[4,18,1,256]{3,1,2,0:T(8,128)(2,1)S(1)}, bf16[4,18,1,256]{3,1,2,0:T(8,128)(2,1)S(1)}, u32[]{:S(2)}, u32[]{:S(2)}) collective-permute-start(bf16[4,18,1,256]{3,1,2,0:T(8,128)(2,1)S(1)} %get-tuple-element.122), channel_id=1, source_target_pairs={{0,1},{1,2},{2,3},{4,5},{5,6},{6,7},{8,9},{9,10},{10,11},{12,13},{... | collective-permute-start | bytes 110600 | tf_op jit(solution)/shard_map/ppermute | solution.py:17
  44.9 4.8 %collective-permute-start.5 = (bf16[4,18,1,256]{3,1,2,0:T(8,128)(2,1)S(1)}, bf16[4,18,1,256]{3,1,2,0:T(8,128)(2,1)S(1)}, u32[]{:S(2)}, u32[]{:S(2)}) collective-permute-start(bf16[4,18,1,256]{3,1,2,0:T(8,128)(2,1)S(1)} %get-tuple-element.123), channel_id=1, source_target_pairs={{1,0},{2,1},{3,2},{5,4},{6,5},{7,6},{9,8},{10,9},{11,10},{13,12},{... | collective-permute-start | bytes 110600 | tf_op jit(solution)/shard_map/ppermute | solution.py:19
  51.5 1.1 copy-start.6
  52.6 5.4 %copy-start.3 = (bf16[2,16,32,256]{3,2,1,0:T(8,128)(2,1)S(1)}, bf16[2,16,32,256]{3,2,1,0:T(8,128)(2,1)}, u32[]{:S(2)}) copy-start(bf16[2,16,32,256]{3,2,1,0:T(8,128)(2,1)} %param.6) | copy-start | bytes 1572868
  59.2 91.5 %all-gather.5.cloned.1.call-start = ((), (), s32[]{:S(2)}) async-start(), calls=%async_computation.2 | async-start | bytes 3932160 | tf_op jit(solution)/shard_map/all_gather | solution.py:44
  176.7 50.3 %collective-permute-start.6 = (bf16[2,4,64,4,256]{4,2,1,3,0:T(8,128)(2,1)}, bf16[2,4,64,4,256]{4,2,1,3,0:T(8,128)(2,1)}, u32[]{:S(2)}, u32[]{:S(2)}) collective-permute-start(bf16[2,4,64,4,256]{4,2,1,3,0:T(8,128)(2,1)} %get-tuple-element.120), channel_id=1, source_target_pairs={{0,4},{4,8},{8,12},{12,16},{16,20},{20,24},{24,28},{28,32},{32,36}... | collective-permute-start | bytes 3145736 | tf_op jit(solution)/shard_map/ppermute | solution.py:17
  183.0 48.6 %collective-permute-start.7 = (bf16[2,4,64,4,256]{4,2,1,3,0:T(8,128)(2,1)}, bf16[2,4,64,4,256]{4,2,1,3,0:T(8,128)(2,1)}, u32[]{:S(2)}, u32[]{:S(2)}) collective-permute-start(bf16[2,4,64,4,256]{4,2,1,3,0:T(8,128)(2,1)} %get-tuple-element.121), channel_id=1, source_target_pairs={{4,0},{8,4},{12,8},{16,12},{20,16},{24,20},{28,24},{32,28},{36,32}... | collective-permute-start | bytes 3145736 | tf_op jit(solution)/shard_map/ppermute | solution.py:19
  240.0 4.5 %copy-start.2 = (f32[2,4,4,64,12,64]{3,5,4,2,1,0:T(8,128)}, f32[2,4,4,64,12,64]{3,5,4,2,1,0:T(8,128)S(1)}, u32[]{:S(2)}) copy-start(f32[2,4,4,64,12,64]{3,5,4,2,1,0:T(8,128)S(1)} %get-tuple-element.171) | copy-start | bytes 18874372 | tf_op jit(solution)/shard_map/while
  248.0 8.4 %copy-start.4 = (bf16[2,2,4,64,4,128]{5,3,4,2,0,1:T(8,128)(2,1)S(1)}, bf16[2,2,4,64,4,128]{5,3,4,2,0,1:T(8,128)(2,1)}, u32[]{:S(2)}) copy-start(bf16[2,2,4,64,4,128]{5,3,4,2,0,1:T(8,128)(2,1)} %get-tuple-element.186) | copy-start | bytes 3145732 | tf_op jit(solution)/shard_map/while
  256.5 1.0 copy-start.5
  262.4 4.5 %copy-start.2 = (f32[2,4,4,64,12,64]{3,5,4,2,1,0:T(8,128)}, f32[2,4,4,64,12,64]{3,5,4,2,1,0:T(8,128)S(1)}, u32[]{:S(2)}) copy-start(f32[2,4,4,64,12,64]{3,5,4,2,1,0:T(8,128)S(1)} %get-tuple-element.171) | copy-start | bytes 18874372 | tf_op jit(solution)/shard_map/while
  270.4 8.4 %copy-start.4 = (bf16[2,2,4,64,4,128]{5,3,4,2,0,1:T(8,128)(2,1)S(1)}, bf16[2,2,4,64,4,128]{5,3,4,2,0,1:T(8,128)(2,1)}, u32[]{:S(2)}) copy-start(bf16[2,2,4,64,4,128]{5,3,4,2,0,1:T(8,128)(2,1)} %get-tuple-element.186) | copy-start | bytes 3145732 | tf_op jit(solution)/shard_map/while
  278.9 1.0 copy-start.5
  279.9 23.7 %copy-start.1 = (bf16[3,3,3,256,256]{4,3,2,1,0:T(8,128)(2,1)S(1)}, bf16[3,3,3,256,256]{4,3,2,1,0:T(8,128)(2,1)}, u32[]{:S(2)}) copy-start(bf16[3,3,3,256,256]{4,3,2,1,0:T(8,128)(2,1)} %param.8) | copy-start | bytes 10616836
  282.3 19.0 %all-to-all-start = ((bf16[2,8,64,4,128]{4,2,1,0,3:T(8,128)(2,1)}), bf16[2,8,64,4,128]{4,2,1,0,3:T(8,128)(2,1)}, u32[]{:S(2)}, u32[]{:S(2)}) async-start(bf16[2,8,64,4,128]{4,2,1,0,3:T(8,128)(2,1)} %copy.54), calls=%async_computation | async-start | bytes 2097152 | tf_op jit(solution)/shard_map/all_to_all | solution.py:90
Sparse Core Ops, SparseCore 0:
  59.3 46.8 all-gather.2
  108.1 42.5 all-gather.4
where the time goes:
time: 311 us; the launch traced here: 310 us
  waiting for transfers between devices  154 us (50%)
  local copies, waits for them, and re-layouts  56 us (18%)
  matrix products  35.1 us (11%)
  starting transfers between devices  33.3 us (11%)
  other arithmetic  15.9 us (5%)
  between operations  14.3 us (5%)
    all_gather x1, waiting for transfers between devices, local(): wide = lax.all_gather(block_out, 'wa', axis=2, tiled=True)  46.3 us
    ppermute x4, waiting for transfers between devices, extended(): lax.ppermute(tail, axis, [(i, (i + 1) % count) for i in range(ends)])  42 us
    all_gather x1, waiting for transfers between devices, local(): col_heads = lax.all_gather(qkv_weight, 'ta', axis=1, tiled=True)  33.7 us
    ppermute x4, starting transfers between devices, extended(): lax.ppermute(tail, axis, [(i, (i + 1) % count) for i in range(ends)])  20.1 us
    ppermute x4, waiting for transfers between devices, extended(): lax.ppermute(head, axis, [((i + 1) % count, i) for i in range(ends)])  19 us
    dot_general x2, matrix products, attend(): jnp.einsum('thiajb,tjbhd->tiahd', probs, value_part, preferred_element_ty...  16.7 us
    all_to_all x1, waiting for transfers between devices, local(): lax.all_to_all(attended, 'ta', split_axis=3, concat_axis=0, tiled=True)  12.7 us
    while x12, local copies, waits for them, and re-layouts  11 us
  transfers between devices with their start and end apart: 11, of which 10 were waited for; matrix products, arithmetic and copies ran while one was open for 5% of the time, Pallas kernels for 0%

commit v1 on v0

--- a/solution.py
+++ b/solution.py
@@ -41,7 +41,10 @@
     )[0]
     block_out = (latent_f32 + conv_out).astype(jnp.bfloat16)
     width_in, head_dev, qkv_count, head_size = qkv_weight.shape
-    col_heads = lax.all_gather(qkv_weight, "ta", axis=1, tiled=True)
+    count_2 = lax.axis_size("ta")
+    pieces = jnp.stack([qkv_weight for _ in range(count_2)])
+    pieces = lax.all_to_all(pieces, "ta", split_axis=0, concat_axis=0)
+    col_heads = jnp.concatenate(pieces, axis=1)
     heads = col_heads.shape[1]
     wide = lax.all_gather(block_out, "wa", axis=2, tiled=True)
     patch_cols = wide.shape[2] // 2

time: 311 us -> 274 us (0.88)
  the two profiles are of different devices: /device:TPU:67 before, /device:TPU:5 now
where the time goes in v1:
time: 274 us
  waiting for transfers between devices  114 us (42%)
  local copies, waits for them, and re-layouts  53.8 us (20%)
  starting transfers between devices  38.8 us (14%)
  matrix products  35.1 us (13%)
  other arithmetic  15.9 us (6%)
  between operations  14.3 us (5%)
    ppermute x4, waiting for transfers between devices, extended(): lax.ppermute(tail, axis, [(i, (i + 1) % count) for i in range(ends)])  43.3 us
    all_gather x1, waiting for transfers between devices, local(): wide = lax.all_gather(block_out, 'wa', axis=2, tiled=True)  39.3 us
    ppermute x4, starting transfers between devices, extended(): lax.ppermute(tail, axis, [(i, (i + 1) % count) for i in range(ends)])  23.1 us
    ppermute x4, waiting for transfers between devices, extended(): lax.ppermute(head, axis, [((i + 1) % count, i) for i in range(ends)])  19.1 us
    dot_general x2, matrix products, attend(): jnp.einsum('thiajb,tjbhd->tiahd', probs, value_part, preferred_element_ty...  16.7 us
    all_to_all x1, waiting for transfers between devices, local(): lax.all_to_all(attended, 'ta', split_axis=3, concat_axis=0, tiled=True)  12.4 us
    while x12, local copies, waits for them, and re-layouts  11 us
    dot_general x2, matrix products, attend(): jnp.einsum('tiahd,tjbhd->thiajb', q_block, key_part, preferred_element_ty...  7.39 us
  transfers between devices with their start and end apart: 11, of which 9 were waited for; matrix products, arithmetic and copies ran while one was open for 7% of the time, Pallas kernels for 0%

profile of v1, /device:TPU:5, one launch (start us, length us, event | category | flops | bytes accessed | tf_op | source)
XLA Modules:
  0.0 273.6 jit_solution(14102131641881272047)
XLA Ops:
  18.6 3.8 %collective-permute-done.1 = bf16[1,16,32,256]{3,1,2,0:T(8,128)(2,1)S(1)} collective-permute-done((bf16[1,16,32,256]{3,1,2,0:T(8,128)(2,1)S(1)}, bf16[1,16,32,256]{3,1,2,0:T(8,128)(2,1)S(1)}, u32[]{:S(2)}, u32[]{:S(2)}) %collective-permute-start.1) | collective-permute-done | bytes 262176 | tf_op jit(solution)/shard_map/ppermute | solution.py:19
  22.6 10.5 %collective-permute-start.2 = (bf16[4,1,32,256]{3,1,2,0:T(2,128)(2,1)S(1)}, bf16[4,1,32,256]{3,1,2,0:T(2,128)(2,1)S(1)}, u32[]{:S(2)}, u32[]{:S(2)}) collective-permute-start(bf16[4,1,32,256]{3,1,2,0:T(2,128)(2,1)S(1)} %get-tuple-element.124), channel_id=1, source_target_pairs={{0,4},{4,8},{8,12},{12,16},{16,20},{20,24},{24,28},{28,32},{32,36}... | collective-permute-start | bytes 196616 | tf_op jit(solution)/shard_map/ppermute | solution.py:17
  37.3 6.1 %collective-permute-done.3 = bf16[4,1,32,256]{3,1,2,0:T(2,128)(2,1)S(1)} collective-permute-done((bf16[4,1,32,256]{3,1,2,0:T(2,128)(2,1)S(1)}, bf16[4,1,32,256]{3,1,2,0:T(2,128)(2,1)S(1)}, u32[]{:S(2)}, u32[]{:S(2)}) %collective-permute-start.3) | collective-permute-done | bytes 65568 | tf_op jit(solution)/shard_map/ppermute | solution.py:19
  47.4 4.2 %collective-permute-done.5 = bf16[4,18,1,256]{3,1,2,0:T(8,128)(2,1)S(1)} collective-permute-done((bf16[4,18,1,256]{3,1,2,0:T(8,128)(2,1)S(1)}, bf16[4,18,1,256]{3,1,2,0:T(8,128)(2,1)S(1)}, u32[]{:S(2)}, u32[]{:S(2)}) %collective-permute-start.5) | collective-permute-done | bytes 36896 | tf_op jit(solution)/shard_map/ppermute | solution.py:19
  54.4 5.0 %fusion.23 = f32[2,16,8,5,256]{4,2,3,1,0:T(8,128)S(1)} fusion(bf16[3,3,3,256,256]{4,3,2,1,0:T(8,128)(2,1)S(1)} %copy-done, bf16[4,18,1,7,2,256]{5,3,4,1,0,2:T(8,128)(2,1)S(1)} %slice.56, bf16[4,18,1,8,5,256]{5,3,4,1,0,2:T(8,128)(2,1)S(1)} %copy.45, pred[8,5]{0,1:T(8,128)(4,1)S(1)} %copy-done.7), kind=kOutput, calls=%fused_computation.40 | convolution fusion | flops 4536369152 | bytes 6840360 | tf_op jit(solution)/shard_map/conv_general_dilated | solution.py:34
  63.4 4.8 %all-to-all-start = ((bf16[4,1024,1,3,128]{1,4,3,2,0:T(8,128)(2,1)}), bf16[4,1024,1,3,128]{1,4,3,2,0:T(8,128)(2,1)}, u32[]{:S(2)}, u32[]{:S(2)}) async-start(bf16[4,1024,1,3,128]{1,4,3,2,0:T(8,128)(2,1)} %stack.2), calls=%async_computation | async-start | bytes 6291456 | tf_op jit(solution)/shard_map/all_to_all | solution.py:46
  68.3 39.3 %all-gather.2.cloned.1.call-done = bf16[2,16,128,256]{3,1,2,0:T(8,128)(2,1)} async-done(((bf16[2,16,32,256]{3,1,2,0:T(8,128)(2,1)}), bf16[2,16,128,256]{3,1,2,0:T(8,128)(2,1)}) %all-gather.2.cloned.1.call-update) | async-done | bytes 2097168 | tf_op jit(solution)/shard_map/all_gather | solution.py:49
  113.9 4.5 %reshape.108 = bf16[1024,1024]{1,0:T(8,128)(2,1)} reshape(bf16[2,8,64,2,2,256]{5,4,3,2,1,0:T(2,128)(2,1)} %bitcast.93) | data formatting | bytes 4194304 | tf_op jit(solution)/shard_map/reshape | solution.py:54
  118.4 6.0 %convolution_convert_fusion = bf16[1024,1536]{1,0:T(8,128)(2,1)S(1)} fusion(bf16[1024,1024]{1,0:T(8,128)(2,1)} %reshape.108, bf16[1024,1536]{0,1:T(8,128)(2,1)} %bitcast.20), kind=kOutput, calls=%fused_computation.28 | convolution fusion | flops 3222798336 | bytes 8388608 | tf_op jit(solution)/shard_map/dot_general | solution.py:56
  124.4 4.5 %reshape.110 = bf16[2,8,64,4,3,128]{5,4,3,2,1,0:T(4,128)(2,1)} reshape(bf16[1024,1536]{1,0:T(8,128)(2,1)S(1)} %convolution_convert_fusion) | data formatting | bytes 6291456 | tf_op jit(solution)/shard_map/reshape | solution.py:59
  128.9 4.6 %slice.58 = bf16[2,8,64,4,2,128]{5,4,3,2,1,0:T(2,128)(2,1)S(1)} slice(bf16[2,8,64,4,3,128]{5,4,3,2,1,0:T(4,128)(2,1)} %reshape.110), slice={[0:2], [0:8], [0:64], [0:4], [1:3], [0:128]} | slice | bytes 4194304 | tf_op jit(solution)/shard_map/slice | solution.py:61
  139.8 6.7 %collective-permute-start.6 = (bf16[2,4,64,4,256]{4,2,1,3,0:T(8,128)(2,1)}, bf16[2,4,64,4,256]{4,2,1,3,0:T(8,128)(2,1)}, u32[]{:S(2)}, u32[]{:S(2)}) collective-permute-start(bf16[2,4,64,4,256]{4,2,1,3,0:T(8,128)(2,1)} %get-tuple-element.120), channel_id=1, source_target_pairs={{0,4},{4,8},{8,12},{12,16},{16,20},{20,24},{24,28},{28,32},{32,36}... | collective-permute-start | bytes 3145736 | tf_op jit(solution)/shard_map/ppermute | solution.py:17
  148.7 3.8 %slice.61 = bf16[2,8,64,4,1,128]{5,4,3,2,1,0:T(2,128)(2,1)S(1)} slice(bf16[2,8,64,4,3,128]{5,4,3,2,1,0:T(4,128)(2,1)} %reshape.110), slice={[0:2], [0:8], [0:64], [0:4], [0:1], [0:128]} | slice | bytes 2097152 | tf_op jit(solution)/shard_map/slice | solution.py:60
  152.7 37.4 %collective-permute-done.6 = bf16[2,4,64,4,256]{4,2,1,3,0:T(8,128)(2,1)} collective-permute-done((bf16[2,4,64,4,256]{4,2,1,3,0:T(8,128)(2,1)}, bf16[2,4,64,4,256]{4,2,1,3,0:T(8,128)(2,1)}, u32[]{:S(2)}, u32[]{:S(2)}) %collective-permute-start.6) | collective-permute-done | bytes 1048608 | tf_op jit(solution)/shard_map/ppermute | solution.py:17
  190.2 5.0 %collective-permute-done.7 = bf16[2,4,64,4,256]{4,2,1,3,0:T(8,128)(2,1)} collective-permute-done((bf16[2,4,64,4,256]{4,2,1,3,0:T(8,128)(2,1)}, bf16[2,4,64,4,256]{4,2,1,3,0:T(8,128)(2,1)}, u32[]{:S(2)}, u32[]{:S(2)}) %collective-permute-start.7) | collective-permute-done | bytes 1048608 | tf_op jit(solution)/shard_map/ppermute | solution.py:19
  198.5 44.8 %while.12 = (s32[]{:T(128)}, bf16[2,2,4,64,4,128]{5,3,4,2,0,1:T(8,128)(2,1)}, s32[2]{0:T(128)S(1)}, bf16[2,16,64,4,256]{4,2,1,3,0:T(8,128)(2,1)}, s32[]{:T(128)}...) while((s32[]{:T(128)}, ...), condition=%wide.region_4.5_spmd, body=%wide.region_1.4_spmd.sunk | while | flops 824439104 | bytes 64005228 | solution.py:89
  199.8 3.7 %fusion.49 = (f32[2,4,4,64]{3,2,1,0:T(4,128)S(1)}, f32[2,4,4,64,12,64]{3,5,4,2,1,0:T(8,128)S(1)}) fusion(pred[4,12]{1,0:T(4,128)(4,1)S(1)} %fusion.48, bf16[2,16,64,4,256]{4,2,1,3,0:T(8,128)(2,1)} %get-tuple-element.200, s32[]{:T(128)S(6)} %select_n.43, bf16[2,8,64,4,128]{4,2,1,3,0:T(8,128)(2,1)S(1)} %get-tuple-element.202, s32[]{:T(128)S(6)} %select_n.44), kind=kOutput, calls=%fused_computation.3.clone.1 | convolution fusion | flops 407369728 | bytes 8397320 | tf_op jit(solution)/shard_map/while/body/eval_jaxpr/tiahd,tjbhd->thiajb/dot_general | solution.py:73
  203.5 4.5 %copy-done.2 = f32[2,4,4,64,12,64]{3,5,4,2,1,0:T(8,128)} copy-done((f32[2,4,4,64,12,64]{3,5,4,2,1,0:T(8,128)}, f32[2,4,4,64,12,64]{3,5,4,2,1,0:T(8,128)S(1)}, u32[]{:S(2)}) %copy-start.2) | copy-done | bytes 6291480 | tf_op jit(solution)/shard_map/while
  211.5 8.4 %fusion.51 = bf16[1,2,4,64,4,128]{5,3,2,4,1,0:T(8,128)(2,1)S(1)} fusion(f32[2,4,4,64,12,64]{3,5,4,2,1,0:T(8,128)} %copy-done.2, f32[2,4,4,64]{3,2,1,0:T(4,128)S(1)} %fusion.50, f32[2,4,4,64]{3,2,1,0:T(4,128)S(1)} %get-tuple-element.172, pred[4,12]{1,0:T(4,128)(4,1)S(1)} %fusion.48, bf16[2,16,64,4,256]{4,2,1,3,0:T(8,128)(2,1)} %get-tuple-element.200, ...), kind=kOutput, calls=%fused_computation.11.clone.1 | convolution fusion | flops 410779648 | bytes 14696504 | tf_op jit(solution)/shard_map/while/body/eval_jaxpr/thiajb,tjbhd->tiahd/dot_general | solution.py:84
  222.2 3.7 %fusion.49 = (f32[2,4,4,64]{3,2,1,0:T(4,128)S(1)}, f32[2,4,4,64,12,64]{3,5,4,2,1,0:T(8,128)S(1)}) fusion(pred[4,12]{1,0:T(4,128)(4,1)S(1)} %fusion.48, bf16[2,16,64,4,256]{4,2,1,3,0:T(8,128)(2,1)} %get-tuple-element.200, s32[]{:T(128)S(6)} %select_n.43, bf16[2,8,64,4,128]{4,2,1,3,0:T(8,128)(2,1)S(1)} %get-tuple-element.202, s32[]{:T(128)S(6)} %select_n.44), kind=kOutput, calls=%fused_computation.3.clone.1 | convolution fusion | flops 407369728 | bytes 8397320 | tf_op jit(solution)/shard_map/while/body/eval_jaxpr/tiahd,tjbhd->thiajb/dot_general | solution.py:73
  225.9 4.5 %copy-done.2 = f32[2,4,4,64,12,64]{3,5,4,2,1,0:T(8,128)} copy-done((f32[2,4,4,64,12,64]{3,5,4,2,1,0:T(8,128)}, f32[2,4,4,64,12,64]{3,5,4,2,1,0:T(8,128)S(1)}, u32[]{:S(2)}) %copy-start.2) | copy-done | bytes 6291480 | tf_op jit(solution)/shard_map/while
  233.9 8.4 %fusion.51 = bf16[1,2,4,64,4,128]{5,3,2,4,1,0:T(8,128)(2,1)S(1)} fusion(f32[2,4,4,64,12,64]{3,5,4,2,1,0:T(8,128)} %copy-done.2, f32[2,4,4,64]{3,2,1,0:T(4,128)S(1)} %fusion.50, f32[2,4,4,64]{3,2,1,0:T(4,128)S(1)} %get-tuple-element.172, pred[4,12]{1,0:T(4,128)(4,1)S(1)} %fusion.48, bf16[2,16,64,4,256]{4,2,1,3,0:T(8,128)(2,1)} %get-tuple-element.200, ...), kind=kOutput, calls=%fused_computation.11.clone.1 | convolution fusion | flops 410779648 | bytes 14696504 | tf_op jit(solution)/shard_map/while/body/eval_jaxpr/thiajb,tjbhd->tiahd/dot_general | solution.py:84
  245.8 4.2 %all-to-all-start.1 = ((bf16[2,8,64,4,128]{4,2,1,0,3:T(8,128)(2,1)}), bf16[2,8,64,4,128]{4,2,1,0,3:T(8,128)(2,1)}, u32[]{:S(2)}, u32[]{:S(2)}) async-start(bf16[2,8,64,4,128]{4,2,1,0,3:T(8,128)(2,1)} %copy.56), calls=%async_computation.1 | async-start | bytes 2097152 | tf_op jit(solution)/shard_map/all_to_all | solution.py:93
  252.0 12.4 %all-to-all-done.1 = bf16[2,8,64,4,128]{4,2,1,0,3:T(8,128)(2,1)} async-done(((bf16[2,8,64,4,128]{4,2,1,0,3:T(8,128)(2,1)}), bf16[2,8,64,4,128]{4,2,1,0,3:T(8,128)(2,1)}, u32[]{:S(2)}, u32[]{:S(2)}) %all-to-all-start.1) | async-done | bytes 1048608 | tf_op jit(solution)/shard_map/all_to_all | solution.py:93
  (71 shorter events, 61.7 us)
Async XLA Ops:
  7.2 47.2 %copy-start = (bf16[3,3,3,256,256]{4,3,2,1,0:T(8,128)(2,1)S(1)}, bf16[3,3,3,256,256]{4,3,2,1,0:T(8,128)(2,1)}, u32[]{:S(2)}) copy-start(bf16[3,3,3,256,256]{4,3,2,1,0:T(8,128)(2,1)} %param.8) | copy-start | bytes 10616836
  7.2 100.4 %all-gather.2.cloned.1.call-start = ((), (), s32[]{:S(2)}) async-start(), calls=%async_computation.2 | async-start | bytes 2621440 | tf_op jit(solution)/shard_map/all_gather | solution.py:49
  10.4 8.2 %collective-permute-start = (bf16[1,16,32,256]{3,1,2,0:T(8,128)(2,1)S(1)}, bf16[1,16,32,256]{3,1,2,0:T(8,128)(2,1)S(1)}, u32[]{:S(2)}, u32[]{:S(2)}) collective-permute-start(bf16[1,16,32,256]{3,1,2,0:T(8,128)(2,1)S(1)} %get-tuple-element.126), channel_id=1, source_target_pairs={{0,64},{64,128},{128,192},{1,65},{65,129},{129,193},{2,66},{66,130... | collective-permute-start | bytes 786440 | tf_op jit(solution)/shard_map/ppermute | solution.py:17
  13.6 8.8 %collective-permute-start.1 = (bf16[1,16,32,256]{3,1,2,0:T(8,128)(2,1)S(1)}, bf16[1,16,32,256]{3,1,2,0:T(8,128)(2,1)S(1)}, u32[]{:S(2)}, u32[]{:S(2)}) collective-permute-start(bf16[1,16,32,256]{3,1,2,0:T(8,128)(2,1)S(1)} %get-tuple-element.127), channel_id=1, source_target_pairs={{64,0},{128,64},{192,128},{65,1},{129,65},{193,129},{66,2},{130,66... | collective-permute-start | bytes 786440 | tf_op jit(solution)/shard_map/ppermute | solution.py:19
  22.6 14.7 %collective-permute-start.2 = (bf16[4,1,32,256]{3,1,2,0:T(2,128)(2,1)S(1)}, bf16[4,1,32,256]{3,1,2,0:T(2,128)(2,1)S(1)}, u32[]{:S(2)}, u32[]{:S(2)}) collective-permute-start(bf16[4,1,32,256]{3,1,2,0:T(2,128)(2,1)S(1)} %get-tuple-element.124), channel_id=1, source_target_pairs={{0,4},{4,8},{8,12},{12,16},{16,20},{20,24},{24,28},{28,32},{32,36}... | collective-permute-start | bytes 196616 | tf_op jit(solution)/shard_map/ppermute | solution.py:17
  33.1 10.3 %collective-permute-start.3 = (bf16[4,1,32,256]{3,1,2,0:T(2,128)(2,1)S(1)}, bf16[4,1,32,256]{3,1,2,0:T(2,128)(2,1)S(1)}, u32[]{:S(2)}, u32[]{:S(2)}) collective-permute-start(bf16[4,1,32,256]{3,1,2,0:T(2,128)(2,1)S(1)} %get-tuple-element.125), channel_id=1, source_target_pairs={{4,0},{8,4},{12,8},{16,12},{20,16},{24,20},{28,24},{32,28},{36,32}... | collective-permute-start | bytes 196616 | tf_op jit(solution)/shard_map/ppermute | solution.py:19
  43.5 3.9 %collective-permute-start.4 = (bf16[4,18,1,256]{3,1,2,0:T(8,128)(2,1)S(1)}, bf16[4,18,1,256]{3,1,2,0:T(8,128)(2,1)S(1)}, u32[]{:S(2)}, u32[]{:S(2)}) collective-permute-start(bf16[4,18,1,256]{3,1,2,0:T(8,128)(2,1)S(1)} %get-tuple-element.122), channel_id=1, source_target_pairs={{0,1},{1,2},{2,3},{4,5},{5,6},{6,7},{8,9},{9,10},{10,11},{12,13},{... | collective-permute-start | bytes 110600 | tf_op jit(solution)/shard_map/ppermute | solution.py:17
  46.1 5.5 %collective-permute-start.5 = (bf16[4,18,1,256]{3,1,2,0:T(8,128)(2,1)S(1)}, bf16[4,18,1,256]{3,1,2,0:T(8,128)(2,1)S(1)}, u32[]{:S(2)}, u32[]{:S(2)}) collective-permute-start(bf16[4,18,1,256]{3,1,2,0:T(8,128)(2,1)S(1)} %get-tuple-element.123), channel_id=1, source_target_pairs={{1,0},{2,1},{3,2},{5,4},{6,5},{7,6},{9,8},{10,9},{11,10},{13,12},{... | collective-permute-start | bytes 110600 | tf_op jit(solution)/shard_map/ppermute | solution.py:19
  53.3 1.1 copy-start.7
  54.4 5.4 %copy-start.3 = (bf16[2,16,32,256]{3,2,1,0:T(8,128)(2,1)S(1)}, bf16[2,16,32,256]{3,2,1,0:T(8,128)(2,1)}, u32[]{:S(2)}) copy-start(bf16[2,16,32,256]{3,2,1,0:T(8,128)(2,1)} %param.6) | copy-start | bytes 1572868
  59.4 1.6 copy-start.6
  63.4 54.9 %all-to-all-start = ((bf16[4,1024,1,3,128]{1,4,3,2,0:T(8,128)(2,1)}), bf16[4,1024,1,3,128]{1,4,3,2,0:T(8,128)(2,1)}, u32[]{:S(2)}, u32[]{:S(2)}) async-start(bf16[4,1024,1,3,128]{1,4,3,2,0:T(8,128)(2,1)} %stack.2), calls=%async_computation | async-start | bytes 6291456 | tf_op jit(solution)/shard_map/all_to_all | solution.py:46
  139.8 50.4 %collective-permute-start.6 = (bf16[2,4,64,4,256]{4,2,1,3,0:T(8,128)(2,1)}, bf16[2,4,64,4,256]{4,2,1,3,0:T(8,128)(2,1)}, u32[]{:S(2)}, u32[]{:S(2)}) collective-permute-start(bf16[2,4,64,4,256]{4,2,1,3,0:T(8,128)(2,1)} %get-tuple-element.120), channel_id=1, source_target_pairs={{0,4},{4,8},{8,12},{12,16},{16,20},{20,24},{24,28},{28,32},{32,36}... | collective-permute-start | bytes 3145736 | tf_op jit(solution)/shard_map/ppermute | solution.py:17
  146.5 48.6 %collective-permute-start.7 = (bf16[2,4,64,4,256]{4,2,1,3,0:T(8,128)(2,1)}, bf16[2,4,64,4,256]{4,2,1,3,0:T(8,128)(2,1)}, u32[]{:S(2)}, u32[]{:S(2)}) collective-permute-start(bf16[2,4,64,4,256]{4,2,1,3,0:T(8,128)(2,1)} %get-tuple-element.121), channel_id=1, source_target_pairs={{4,0},{8,4},{12,8},{16,12},{20,16},{24,20},{28,24},{32,28},{36,32}... | collective-permute-start | bytes 3145736 | tf_op jit(solution)/shard_map/ppermute | solution.py:19
  203.5 4.5 %copy-start.2 = (f32[2,4,4,64,12,64]{3,5,4,2,1,0:T(8,128)}, f32[2,4,4,64,12,64]{3,5,4,2,1,0:T(8,128)S(1)}, u32[]{:S(2)}) copy-start(f32[2,4,4,64,12,64]{3,5,4,2,1,0:T(8,128)S(1)} %get-tuple-element.171) | copy-start | bytes 18874372 | tf_op jit(solution)/shard_map/while
  211.5 8.4 %copy-start.4 = (bf16[2,2,4,64,4,128]{5,3,4,2,0,1:T(8,128)(2,1)S(1)}, bf16[2,2,4,64,4,128]{5,3,4,2,0,1:T(8,128)(2,1)}, u32[]{:S(2)}) copy-start(bf16[2,2,4,64,4,128]{5,3,4,2,0,1:T(8,128)(2,1)} %get-tuple-element.186) | copy-start | bytes 3145732 | tf_op jit(solution)/shard_map/while
  220.0 1.0 copy-start.5
  225.9 4.5 %copy-start.2 = (f32[2,4,4,64,12,64]{3,5,4,2,1,0:T(8,128)}, f32[2,4,4,64,12,64]{3,5,4,2,1,0:T(8,128)S(1)}, u32[]{:S(2)}) copy-start(f32[2,4,4,64,12,64]{3,5,4,2,1,0:T(8,128)S(1)} %get-tuple-element.171) | copy-start | bytes 18874372 | tf_op jit(solution)/shard_map/while
  233.9 8.4 %copy-start.4 = (bf16[2,2,4,64,4,128]{5,3,4,2,0,1:T(8,128)(2,1)S(1)}, bf16[2,2,4,64,4,128]{5,3,4,2,0,1:T(8,128)(2,1)}, u32[]{:S(2)}) copy-start(bf16[2,2,4,64,4,128]{5,3,4,2,0,1:T(8,128)(2,1)} %get-tuple-element.186) | copy-start | bytes 3145732 | tf_op jit(solution)/shard_map/while
  242.4 1.0 copy-start.5
  243.3 23.4 %copy-start.1 = (bf16[3,3,3,256,256]{4,3,2,1,0:T(8,128)(2,1)S(1)}, bf16[3,3,3,256,256]{4,3,2,1,0:T(8,128)(2,1)}, u32[]{:S(2)}) copy-start(bf16[3,3,3,256,256]{4,3,2,1,0:T(8,128)(2,1)} %param.8) | copy-start | bytes 10616836
  245.8 18.7 %all-to-all-start.1 = ((bf16[2,8,64,4,128]{4,2,1,0,3:T(8,128)(2,1)}), bf16[2,8,64,4,128]{4,2,1,0,3:T(8,128)(2,1)}, u32[]{:S(2)}, u32[]{:S(2)}) async-start(bf16[2,8,64,4,128]{4,2,1,0,3:T(8,128)(2,1)} %copy.56), calls=%async_computation.1 | async-start | bytes 2097152 | tf_op jit(solution)/shard_map/all_to_all | solution.py:93
Sparse Core Ops, SparseCore 0:
  61.2 46.3 all-gather.1
